TPU v7x, 32 devices: a whole 2x2x4 slice. The times are simulated.
32 devices in a mesh: tx: 8 (over y, x, core), ty: 4 (over z).
Axes of the slice: x: 2, y: 2, z: 4, core: 2. Of those that a mesh axis runs over, the one named last changes fastest.
Arguments:
- offsets: float32 [2, 16, 16, 128], P(None, 'tx', 'ty'), may hold values from 0 to 1
- circ: float32 [16, 16, 128], P('tx', 'ty'), as said below
- counts: int32 [16, 16], P('tx', 'ty'), may hold values from 1 to 128, as said below
Outputs:
- velocity: float32 [2, 16, 16, 128], P(None, 'tx', 'ty')
- moved: float32 [2, 16, 16, 128], P(None, 'tx', 'ty')
Inputs may be any that keep to these rules, and one draw needn't show every extreme that they name: counts of live slots in each cell; at least one cell holds 128; the middle quarter of the cell rows holds more on average. `circ`: circulations of order 0.02 / sqrt(128), of both signs.
All inputs are finite; a program needn't handle non-finite values.
Results may differ from a plain program's by a relative error of at most 0.00011.
Values sent between devices are 32-bit elements; how exact they have to be, the bound alone decides.
No kernel may reach another device: no remote copies, remote signals or barrier semaphores. Data moves between devices by JAX's collectives and lax.ppermute only.
A program may use at most 64 MiB of HBM per device.

v0:
```python
import functools
import math

import jax
import jax.numpy as jnp
from jax import lax
from jax.experimental import pallas as pl
from jax.experimental.pallas import tpu as pltpu
from jax.sharding import PartitionSpec as P


MODES = 64
HALF = MODES // 2

two_pi = 2.0 * math.pi
screen = 1.5625
smooth = 0.0625
section_step = 0.25
unit = math.sqrt(screen / math.log(2.0))
floor_term = smooth * unit * unit

VMEM = pl.BlockSpec(memory_space=pltpu.VMEM)
PARAMS = pltpu.CompilerParams(vmem_limit_bytes=8 * 1024 * 1024)


def position():
    tx = lax.axis_index("tx")
    return tx, lax.axis_index("ty"), lax.rem(tx, 2)


def call(body, out_shapes, scratch, flops, *args):
    outs = [jax.ShapeDtypeStruct(s, d) for s, d in out_shapes]
    return pl.pallas_call(
        body,
        out_shape=outs,
        in_specs=[VMEM] * len(args),
        out_specs=[VMEM] * len(outs),
        scratch_shapes=scratch,
        compiler_params=PARAMS,
        cost_estimate=pl.CostEstimate(flops=flops, bytes_accessed=65536, transcendentals=0),
    )(*args)


def unit_circle(turn):
    quarter = jnp.floor(4.0 * turn + 0.5)
    angle = two_pi * (turn - 0.25 * quarter)
    sq = angle * angle
    sine = angle * (
        1.0 + sq * (-1.0 / 6 + sq * (1.0 / 120 + sq * (-1.0 / 5040 + sq * (1.0 / 362880))))
    )
    cosine = 1.0 + sq * (
        -0.5 + sq * (1.0 / 24 + sq * (-1.0 / 720 + sq * (1.0 / 40320 + sq * (-1.0 / 3628800))))
    )
    odd = (quarter == 1.0) | (quarter == 3.0)
    cos_neg = (quarter == 1.0) | (quarter == 2.0)
    sin_neg = (quarter == 2.0) | (quarter == 3.0)
    cos_part = jnp.where(odd, sine, cosine)
    sin_part = jnp.where(odd, cosine, sine)
    return jnp.where(cos_neg, -cos_part, cos_part), jnp.where(sin_neg, -sin_part, sin_part)


def times(p, q):
    return p[0] * q[0] - p[1] * q[1], p[0] * q[1] + p[1] * q[0]


def split(value):
    high = value.astype(jnp.bfloat16)
    low = (value - high.astype(jnp.float32)).astype(jnp.bfloat16)
    return high, low


def moments_kernel(
    rows, cols, cell_count, corner, offsets, counts, circ, own, kept, x_table, y_table,
    powers, amounts,
):
    cells = rows * cols
    slots = circ.shape[2]
    shape = (cells, slots)
    place = position()
    cell = lax.broadcasted_iota(jnp.int32, shape, 0)
    row_in = jnp.zeros(shape, jnp.int32)
    for r in range(1, rows):
        row_in = jnp.where(cell >= r * cols, r, row_in)
    col_in = cell - row_in * cols
    slot = lax.broadcasted_iota(jnp.int32, (1, slots), 1)
    for r in range(rows):
        cells_of = pl.ds(r * cols, cols)
        kept[0, cells_of, :] = offsets[0, r]
        kept[1, cells_of, :] = offsets[1, r]
        for c in range(cols):
            count = jnp.broadcast_to(counts[pl.ds(r, 1), pl.ds(c, 1)], (1, slots))
            kept[3, pl.ds(r * cols + c, 1), :] = jnp.where(slot < count, 1.0, 0.0)
        kept[2, cells_of, :] = jnp.where(kept[3, cells_of, :] > 0.5, circ[r], 0.0)
    off_x, off_y, strength = kept[0], kept[1], kept[2]
    x_turn = ((corner[pl.ds(0, 1), :] + col_in.astype(jnp.float32)) + off_x) / cell_count
    y_turn = ((corner[pl.ds(1, 1), :] + row_in.astype(jnp.float32)) + off_y) / cell_count
    own[4] = unit * (col_in.astype(jnp.float32) + off_x)
    own[5] = unit * ((place[2] * rows + row_in).astype(jnp.float32) + off_y)
    own[6] = strength * (unit * cell_count / two_pi)
    amounts[...] = strength
    for axis, turn in ((0, x_turn), (1, y_turn)):
        one = unit_circle(turn)
        two = times(one, one)
        three = times(two, one)
        four = times(two, two)
        low_modes = [
            (jnp.ones(shape, jnp.float32), jnp.zeros(shape, jnp.float32)),
            one, two, three, four, times(four, one), times(four, two), times(four, three),
        ]
        eight = times(four, four)
        for k, point in enumerate(low_modes + [eight, times(eight, eight)]):
            for part in range(2):
                powers[axis, part, k * cells : (k + 1) * cells] = point[part]
    full = None
    pair = 2 if cells % 2 == 0 else 1
    for i in range(0, cells, pair):
        left, right = [], []
        for cell_at in range(i, i + pair):
            lanes = pl.ds(cell_at * slots, slots)
            amount = jnp.broadcast_to(amounts[pl.ds(cell_at, 1), :], (8, slots))
            for axis, table, parts in ((0, x_table, left), (1, y_table, right)):

                def row(k, part):
                    at = pl.ds(k * cells + cell_at, 1)
                    return jnp.broadcast_to(powers[axis, part, at, :], (8, slots))

                group = tuple(
                    powers[axis, part, pl.ds(cell_at, 8, stride=cells), :] for part in range(2)
                )
                second = times(group, (row(8, 0), row(8, 1)))
                sixteen = (row(9, 0), row(9, 1))
                groups = [group, second, times(group, sixteen), times(second, sixteen)]
                wave = [g[0] for g in groups] + [g[1] for g in groups]
                table[:, lanes] = jnp.concatenate(wave, axis=0)
                if axis == 0:
                    wave = [piece * amount for piece in wave]
                parts.append(jnp.concatenate(split(jnp.concatenate(wave, axis=0)), axis=0))
        product = lax.dot_general(
            jnp.concatenate(left, axis=1),
            jnp.concatenate(right, axis=1),
            (((1,), (1,)), ((), ())),
            preferred_element_type=jnp.float32,
        )
        full = product if full is None else full + product
    full = full[0:MODES] + full[MODES : 2 * MODES]
    full = full + pltpu.roll(full, MODES, 1)
    lane = lax.broadcasted_iota(jnp.int32, (HALF, 2 * MODES), 1)
    own[0:4] = jnp.where(lane < MODES, full[0:HALF], full[HALF:MODES]).reshape(4, 8, 2 * MODES)


def pair_terms(target, source, total):
    offset_x = target[0] - source[0]
    offset_y = target[1] - source[1]
    square = offset_x * offset_x + offset_y * offset_y
    weight = source[2] / ((square + floor_term) * jnp.exp2(square))
    return total[0] - offset_y * weight, total[1] + offset_x * weight


def near_sum(sources, targets, links, turned, most=48):
    slots = sources[0][0].shape[1]
    stack = [part for source in sources for part in source]
    pad = -len(stack) % 8
    stack = jnp.concatenate(stack + [jnp.zeros((pad, slots), jnp.float32)] * (pad > 0), axis=0)
    turned[:, 0 : stack.shape[0]] = stack.T
    spread = [tuple(jnp.broadcast_to(part, (8, slots)) for part in t) for t in targets]

    def step(k, totals):
        totals = list(totals)
        chunk = turned[pl.ds(8 * k if isinstance(k, int) else pl.multiple_of(8 * k, 8), 8), :]
        for i, reached in enumerate(links):
            source = tuple(
                jnp.broadcast_to(chunk[:, 3 * i + part : 3 * i + part + 1], (8, slots))
                for part in range(3)
            )
            for t in reached:
                totals[2 * t], totals[2 * t + 1] = pair_terms(
                    spread[t], source, (totals[2 * t], totals[2 * t + 1])
                )
        return tuple(totals)

    zero = jnp.zeros((8, slots), jnp.float32)
    pairs = sum(len(reached) for reached in links)
    chunks = slots // 8
    group = 1
    while group * 2 * pairs <= most and chunks % (group * 2) == 0:
        group *= 2

    def grouped(k, totals):
        for u in range(group):
            totals = step(k * group + u, totals)
        return totals

    totals = (zero,) * (2 * len(targets))
    if group == chunks:
        totals = grouped(0, totals)
    else:
        totals = lax.fori_loop(0, chunks // group, grouped, totals)
    return [jnp.sum(total, axis=0, keepdims=True) for total in totals]


def reach(col, cols):
    return [c for c in (col - 1, col, col + 1) if 0 <= c < cols]


def read_row(ref, base, at):
    return tuple(ref[base + part, pl.ds(at, 1), :] for part in range(3))


def near_last_cols(rows, cols, side, spread, right, near):
    slots = side.shape[2]
    shift = jnp.where(right == 1, unit * cols, -unit * cols)
    sources = []
    for k in range(rows + 2):
        row = (
            side[4, pl.ds(k, 1), :] + shift,
            side[4, pl.ds(rows + 2 + k, 1), :],
            side[5, pl.ds(k, 1), :],
        )
        sources.append(tuple(jnp.broadcast_to(part, (8, slots)) for part in row))
    stack = []
    for r in range(rows):
        parts = ([], [])
        for k in range(slots // 8):
            target = tuple(spread[2 * r + part, 8 * k : 8 * k + 8] for part in range(2))
            total = (0.0, 0.0)
            for i in range(r, r + 3):
                total = pair_terms(target, sources[i], total)
            parts[0].append(total[0])
            parts[1].append(total[1])
        stack += parts[0] + parts[1]
    high, low = split(jnp.concatenate(stack, axis=0))
    ones = jnp.ones((8, slots), jnp.bfloat16)

    def lanes_sum(value):
        return lax.dot_general(
            ones, value, (((1,), (1,)), ((), ())), preferred_element_type=jnp.float32
        )

    sums = lanes_sum(high) + lanes_sum(low)
    edge = jnp.where(right == 1, cols - 1, 0)
    for r in range(rows):
        for part in range(2):
            at = pl.ds(r * cols + edge, 1)
            lanes = slice((2 * r + part) * slots, (2 * r + part + 1) * slots)
            near[part, at, :] = near[part, at, :] + sums[0:1, lanes]


def near_local(rows, cols, own, cells, near, turned):
    if not cells:
        return
    places = sorted({(r, c) for row, col in cells for r in range(rows) if abs(r - row) <= 1 for c in reach(col, cols)})
    sources = [read_row(own, 4, r * cols + c) for r, c in cells]
    targets = [read_row(own, 4, r * cols + c)[:2] for r, c in places]
    links = [
        [t for t, (r, c) in enumerate(places) if abs(r - row) <= 1 and abs(c - col) <= 1]
        for row, col in cells
    ]
    sums = near_sum(sources, targets, links, turned)
    for t, (r, c) in enumerate(places):
        for part in range(2):
            at = pl.ds(r * cols + c, 1)
            near[part, at, :] = near[part, at, :] + sums[2 * t + part]


def near_local_kernel(rows, cols, cells, own, near, turned):
    near[...] = jnp.zeros_like(near)
    near_local(rows, cols, own, cells, near, turned)


def near_rows(rows, cols, own, outer, base, above, near, turned):
    def pick(ref, origin, part, first, second):
        return jnp.where(
            above == 1, ref[origin + part, pl.ds(first, 1), :], ref[origin + part, pl.ds(second, 1), :]
        )

    sources = [
        tuple(pick(outer, base, part, cols + c, c) for part in range(3)) for c in range(cols)
    ]
    last = (rows - 1) * cols
    targets = [tuple(pick(own, 4, part, c, last + c) for part in range(2)) for c in range(cols)]
    sums = near_sum(sources, targets, [reach(c, cols) for c in range(cols)], turned)
    top = jnp.where(above == 1, 0, last)
    for c in range(cols):
        for part in range(2):
            at = pl.ds(top + c, 1)
            near[part, at, :] = near[part, at, :] + sums[2 * c + part]


def near_cols(rows, cols, own, side, base, right, near, turned, most=48):
    shift = jnp.where(right == 1, unit * cols, -unit * cols)
    sources = []
    for k in range(rows + 2):
        row = read_row(side, base, k)
        sources.append((row[0] + shift, row[1], row[2]))
    edge = jnp.where(right == 1, cols - 1, 0)
    targets = [read_row(own, 4, r * cols + edge)[:2] for r in range(rows)]
    links = [[r for r in range(rows) if 0 <= k - r <= 2] for k in range(rows + 2)]
    sums = near_sum(sources, targets, links, turned, most)
    for r in range(rows):
        for part in range(2):
            at = pl.ds(r * cols + edge, 1)
            near[part, at, :] = near[part, at, :] + sums[2 * r + part]


def near_partner_kernel(rows, cols, cells, own, partner, near, turned):
    place = position()
    near[...] = jnp.zeros_like(near)
    near_local(rows, cols, own, cells, near, turned)
    near_rows(rows, cols, own, partner, 4, place[2], near, turned)


def near_ring_kernel(rows, cols, own, ring, near, turned):
    place = position()
    near[...] = jnp.zeros_like(near)
    near_rows(rows, cols, own, ring, 0, 1 - place[2], near, turned)


def near_close_kernel(
    rows, cols, cell_count, own, close, y_wave, near, weights, spread, y_table, turned
):
    high, low = split(y_wave[...])
    y_table[0:MODES] = high
    y_table[MODES : 2 * MODES] = low
    shape = (HALF, 2 * MODES)
    lane = lax.broadcasted_iota(jnp.int32, shape, 1)
    m = lax.broadcasted_iota(jnp.int32, shape, 0).astype(jnp.float32)
    n = (lane & (HALF - 1)).astype(jnp.float32)
    square = (two_pi * two_pi) * (m * m + n * n)
    keep = square > 0.0
    safe = jnp.where(keep, square, 1.0)
    damping = jnp.where(keep, jnp.exp(-safe / (6.25 * cell_count * cell_count)) / safe, 0.0)
    damping = damping * (4.0 * two_pi)
    u_weight = damping * n * jnp.where(m == 0.0, 0.5, 1.0)
    v_weight = damping * m * jnp.where(n == 0.0, 0.5, 1.0)
    weights[0] = u_weight
    weights[1] = v_weight
    place = position()
    near[...] = jnp.zeros_like(near)
    right = 1 - lax.rem(place[1], 2)
    slots = own.shape[2]
    edge = jnp.where(right == 1, 0, cols - 1)
    for r in range(rows):
        for part in range(2):
            row = own[4 + part, pl.ds(r * cols + edge, 1), :]
            spread[2 * r + part] = jnp.broadcast_to(row, (slots, slots)).T
    near_cols(rows, cols, own, close, 0, right, near, turned)


def put_row(message, parts):
    message[4] = jnp.concatenate(parts[0:2], axis=0)
    message[5] = jnp.concatenate([parts[2], jnp.zeros_like(parts[2])], axis=0)


def get_row(message, cols):
    return message[4, 0:cols], message[4, cols : 2 * cols], message[5, 0:cols]


def chip_even():
    return lax.rem(lax.div(lax.axis_index("tx"), 2), 2) == 0


def join_kernel(rows, cols, own, partner, message, across, corner):
    core = position()[2]
    last = (rows - 1) * cols
    total = own[0:4] + partner[0:4]
    for target in (message, across, corner):
        target[0:4] = total
    even = chip_even()
    near_parts, far_parts = [], []
    for at in range(4, 7):
        first_row = jnp.where(core == 0, own[at, 0:cols], partner[at, 0:cols])
        last_row = jnp.where(core == 0, partner[at, last:], own[at, last:])
        near_parts.append(jnp.where(even, last_row, first_row))
        far_parts.append(jnp.where(even, first_row, last_row))
    put_row(message, near_parts)
    put_row(corner, far_parts)


def pack_kernel(rows, cols, own, partner, message, near_item, far_item, *others):
    got, (packed, ring) = others[:-2], others[-2:]
    core = position()[2]
    even = chip_even()
    total = message[0:4]
    for item in got:
        total = total + item[0:4]
    packed[0:4] = total
    shift = 2.0 * rows * unit
    for part, (close, distant) in enumerate(zip(get_row(near_item, cols), get_row(far_item, cols))):
        below = jnp.where(even, close, distant)
        above = jnp.where(even, distant, close)
        if part == 1:
            below, above = below + shift, above - shift
        ring[part] = jnp.concatenate([below, above], axis=0)
    near_col = jnp.where(lax.rem(lax.axis_index("ty"), 2) == 0, cols - 1, 0)
    for part in range(3):
        own_of, partner_of = own.at[4 + part], partner.at[4 + part]
        for base, col in ((0, near_col), (rows + 2, cols - 1 - near_col)):

            def cell(ref, r):
                return ref[pl.ds(r * cols + col, 1), :]

            over = ring[part, pl.ds(cols + col, 1), :]
            under = ring[part, pl.ds(col, 1), :]
            mine = [cell(own_of, r) for r in range(rows)]
            other = [cell(partner_of, r) for r in range(rows)]
            if base == 0:
                entries = (
                    [jnp.where(core == 0, mine[-1], over)]
                    + other
                    + [jnp.where(core == 0, under, mine[0])]
                )
            else:
                entries = (
                    [jnp.where(core == 0, over, other[-1])]
                    + mine
                    + [jnp.where(core == 0, other[0], under)]
                )
            for k, entry in enumerate(entries):
                packed[4 + part, pl.ds(base + k, 1), :] = entry


def turn_kernel(rows, packed, got, message, close):
    count = rows + 2
    message[0:4] = packed[0:4] + got[0:4]
    put_row(message, [got[4 + part, count : 2 * count] for part in range(3)])
    for part in range(3):
        close[part, 0:count] = got[4 + part, 0:count]


def final_kernel(
    rows, cols, kept, own, x_table, y_table, message, got, last,
    near_a, near_b, near_c, near_d, near_e, weights, spread, velocity, moved, near, far,
):
    cells = rows * cols
    slots = own.shape[2]
    place = position()
    shape = (HALF, 2 * MODES)
    lane = lax.broadcasted_iota(jnp.int32, shape, 1)
    total = (message[0:4] + got[0:4]).reshape(shape)
    y_odd = (lane & HALF) != 0
    swapped = jnp.where(y_odd, -pltpu.roll(total, HALF, 1), pltpu.roll(total, 2 * MODES - HALF, 1))
    u_part = weights[0] * swapped
    crossed = pltpu.roll(total, MODES, 1)
    v_part = weights[1] * jnp.where(lane < MODES, -crossed, crossed)
    left = []
    for part in (u_part, v_part):
        other = pltpu.roll(part, MODES, 1)
        for doubled in (
            jnp.where(lane < MODES, part, other),
            jnp.where(lane < MODES, other, part),
        ):
            left.append(jnp.concatenate(split(doubled), axis=1))
    left = jnp.concatenate(left, axis=0)
    right = jnp.concatenate([y_table[...], y_table[...]], axis=0)
    terms = jnp.dot(left, right, preferred_element_type=jnp.float32)
    for i in range(cells):
        lanes = slice(i * slots, (i + 1) * slots)
        wave = x_table[:, lanes]
        far[0, pl.ds(i, 1), :] = jnp.sum(terms[0:MODES, lanes] * wave, axis=0, keepdims=True)
        far[1, pl.ds(i, 1), :] = jnp.sum(terms[MODES:, lanes] * wave, axis=0, keepdims=True)
    near[...] = (near_a[...] + near_b[...]) + (near_c[...] + near_d[...]) + near_e[...]
    near_last_cols(rows, cols, last, spread, lax.rem(place[1], 2), near)
    live = kept[3] > 0.5
    for part in range(2):
        value = jnp.where(live, near[part] + far[part], 0.0)
        after = kept[part] + section_step * value
        for r in range(rows):
            velocity[part, r] = value[r * cols : (r + 1) * cols]
            moved[part, r] = after[r * cols : (r + 1) * cols]


def far_item(items, index):
    if len(items) == 3:
        return items[2]
    count = 1 << (len(items) - 1)
    up = jnp.where(index % 2 == 1, (index + 1) % count, (index + count - 1) % count)
    mask = index ^ up
    chosen = items[-1]
    for k in range(2, len(items) - 1):
        chosen = jnp.where(mask == (1 << k) - 1, items[k], chosen)
    return chosen


def per_device(offsets, circ, counts):
    rows, cols, slots = circ.shape
    cells = rows * cols
    tx_size, ty_size = lax.axis_size("tx"), lax.axis_size("ty")
    chips = tx_size // 2
    cell_count = rows * tx_size
    tx, ty = lax.axis_index("tx"), lax.axis_index("ty")
    chip = tx // 2
    f32, bf16 = jnp.float32, jnp.bfloat16
    turned = [pltpu.VMEM((slots, 128), f32)]
    near_shape = [((2, cells, slots), f32)]

    first_cell = jnp.stack([ty * cols, tx * rows, tx]).astype(jnp.int32)
    corner = jnp.broadcast_to(first_cell[:, None], (3, slots)).astype(f32)
    own, kept, x_table, y_wave = call(
        functools.partial(moments_kernel, rows, cols, cell_count),
        [
            ((7, cells, slots), f32),
            ((4, cells, slots), f32),
            ((MODES, cells * slots), f32),
            ((MODES, cells * slots), f32),
        ],
        [
            pltpu.VMEM((2, 2, 10 * cells, slots), f32),
            pltpu.VMEM((cells, slots), f32),
        ],
        4_000_000,
        corner, offsets, counts, circ,
    )

    def swap(message, chip_bit, column_bit, flip=True):
        pairs = [
            (i * ty_size + q, ((i // 2 ^ chip_bit) * 2 + (i + flip) % 2) * ty_size + (q ^ column_bit))
            for i in range(tx_size)
            for q in range(ty_size)
        ]
        return lax.ppermute(message, ("tx", "ty"), pairs)

    def near_call(body, flops, *args):
        return call(body, near_shape, turned, flops, *args)[0]

    whole = [(r, c) for c in range(cols) for r in range(rows)]
    third = len(whole) // 4
    partner = swap(own, 0, 0)
    near_a = near_call(
        functools.partial(near_local_kernel, rows, cols, whole[:third]), 4_000_000, own
    )
    tile = (cells, slots)
    six = ((6,) + tile, f32)
    first, across, corner = call(
        functools.partial(join_kernel, rows, cols), [six, ((4,) + tile, f32), six], [], 50_000,
        own, partner,
    )
    message = first
    items = [message]
    bit = 1
    while True:
        if bit == 1:
            sent = (first, across, corner)
        else:
            sent = (message,) * 3
        steps = (1, 2, 3) if 4 * bit <= chips else (1,)
        arrived = [swap(part, step * bit, 0, bit == 1) for step, part in zip(steps, sent)]
        items += arrived[::2]
        bit *= len(steps) + 1
        if bit >= chips:
            break
        message = jnp.concatenate([message[0:4] + sum(got[0:4] for got in arrived), items[-1][4:6]])
    near_b = near_call(
        functools.partial(near_local_kernel, rows, cols, whole[third : 3 * third]), 9_000_000, own
    )
    near_c = near_call(
        functools.partial(near_partner_kernel, rows, cols, whole[3 * third :]), 9_000_000,
        own, partner,
    )
    packed, ring = call(
        functools.partial(pack_kernel, rows, cols),
        [((7,) + tile, f32), ((3,) + tile, f32)], [], 100_000,
        own, partner, message, items[1], far_item(items, chip), *arrived,
    )
    got = swap(packed, 0, 1)
    near_d = near_call(functools.partial(near_ring_kernel, rows, cols), 5_000_000, own, ring)
    message, close = call(
        functools.partial(turn_kernel, rows), [six, ((3, rows + 2, slots), f32)], [], 50_000,
        packed, got,
    )
    items = [None, message]
    bit = 2
    while True:
        got = swap(message, 0, bit, bit == 2)
        items.append(got)
        bit *= 2
        if bit >= ty_size:
            break
        message = jnp.concatenate([message[0:4] + got[0:4], got[4:6]])
    near_e, weights, spread, y_table = call(
        functools.partial(near_close_kernel, rows, cols, cell_count),
        near_shape + [((2, HALF, 2 * MODES), f32), ((2 * rows, slots, slots), f32),
           ((2 * MODES, cells * slots), bf16)],
        turned, 3_000_000,
        own, close, y_wave,
    )
    return tuple(
        call(
            functools.partial(final_kernel, rows, cols),
            [(offsets.shape, f32)] * 2,
            [pltpu.VMEM((2, cells, slots), f32), pltpu.VMEM((2, cells, slots), f32)],
            4_000_000,
            kept, own, x_table, y_table, message, got, far_item(items, ty),
            near_a, near_b, near_c, near_d, near_e, weights, spread,
        )
    )


def solution(mesh):
    placed = (P(None, "tx", "ty", None), P("tx", "ty", None), P("tx", "ty"))

    return jax.shard_map(
        per_device,
        mesh=mesh,
        in_specs=placed,
        out_specs=(P(None, "tx", "ty", None), P(None, "tx", "ty", None)),
        check_vma=False,
    )
```

profile of v0, /device:TPU:0, one launch (start us, length us, event | category | flops | bytes accessed | tf_op | source)
XLA Modules:
  0.0 22.6 jit_solution(13284715423138865820)
XLA Ops:
  0.7 0.1 add_convert_fusion
  0.7 0.1 broadcast_in_dim.2.corner
  0.8 0.5 %copy-done = f32[2,2,4,128]{3,2,1,0:T(4,128)S(1)} copy-done((f32[2,2,4,128]{3,2,1,0:T(4,128)S(1)}, f32[2,2,4,128]{3,2,1,0:T(4,128)}, u32[]{:S(2)}) %copy-start) | copy-done | bytes 8216
  1.3 0.0 copy-done.1
  1.3 0.1 copy-done.2
  1.4 0.4 %shard_map.50 = (f32[7,8,128]{2,1,0:T(8,128)S(1)}, f32[4,8,128]{2,1,0:T(8,128)S(1)}, f32[64,1024]{1,0:T(8,128)S(1)}, f32[64,1024]{1,0:T(8,128)S(1)}) custom-call(f32[3,128]{1,0:T(4,128)S(1)} %broadcast_in_dim.2.corner, f32[2,2,4,128]{3,2,1,0:T(4,128)S(1)} %copy-done, s32[2,4]{1,0:T(2,128)S(1)} %copy-done.2, f32[2,4,128]{2,1,0:T(4,128)S(1)} %copy-done.1), custom_call_target="tpu_custom_call" | custom-call | flops 4000000 | bytes 65536 | tf_op jit(solution)/shard_map/pallas_call | solution.py:33
  1.8 0.6 %collective-permute-start = (f32[7,8,128]{2,1,0:T(8,128)S(1)}, f32[7,8,128]{2,1,0:T(8,128)S(1)}, u32[]{:S(2)}, u32[]{:S(2)}) collective-permute-start(f32[7,8,128]{2,1,0:T(8,128)S(1)} %get-tuple-element.18.own), channel_id=1, source_target_pairs={{0,4},{1,5},{2,6},{3,7},{4,0},{5,1},{6,2},{7,3},{8,12},{9,13},{10,... | collective-permute-start | bytes 86024 | tf_op jit(solution)/shard_map/ppermute | solution.py:520
  2.4 0.9 %collective-permute-done.partner = f32[7,8,128]{2,1,0:T(8,128)S(1)} collective-permute-done((f32[7,8,128]{2,1,0:T(8,128)S(1)}, f32[7,8,128]{2,1,0:T(8,128)S(1)}, u32[]{:S(2)}, u32[]{:S(2)}) %collective-permute-start) | collective-permute-done | bytes 28704 | tf_op jit(solution)/shard_map/ppermute | solution.py:520
  3.2 2.7 %collective-permute-start.1 = (f32[6,8,128]{2,1,0:T(8,128)S(1)}, f32[6,8,128]{2,1,0:T(8,128)S(1)}, u32[]{:S(2)}, u32[]{:S(2)}) collective-permute-start(f32[6,8,128]{2,1,0:T(8,128)S(1)} %get-tuple-element.20.message), channel_id=1, source_target_pairs={{0,12},{1,13},{2,14},{3,15},{4,8},{5,9},{6,10},{7,11},{8,4},{9,5},... | collective-permute-start | bytes 73736 | tf_op jit(solution)/shard_map/ppermute | solution.py:520
  5.9 1.4 %collective-permute-start.2 = (f32[6,8,128]{2,1,0:T(8,128)S(1)}, f32[6,8,128]{2,1,0:T(8,128)S(1)}, u32[]{:S(2)}, u32[]{:S(2)}) collective-permute-start(f32[6,8,128]{2,1,0:T(8,128)S(1)} %get-tuple-element.21), channel_id=1, source_target_pairs={{0,28},{1,29},{2,30},{3,31},{4,24},{5,25},{6,26},{7,27},{8,20},{9,... | collective-permute-start | bytes 73736 | tf_op jit(solution)/shard_map/ppermute | solution.py:520
  7.3 0.0 collective-permute-start.3
  7.4 3.4 %collective-permute-done.3.others_1_ = f32[4,8,128]{2,1,0:T(8,128)S(1)} collective-permute-done((f32[4,8,128]{2,1,0:T(8,128)S(1)}, f32[4,8,128]{2,1,0:T(8,128)S(1)}, u32[]{:S(2)}, u32[]{:S(2)}) %collective-permute-start.3) | collective-permute-done | bytes 16416 | tf_op jit(solution)/shard_map/ppermute | solution.py:520
  10.8 0.0 collective-permute-done.1.near_item.others_0_
  10.8 0.0 collective-permute-done.2.far_item.others_2_
  10.9 1.4 %collective-permute-start.4 = (f32[7,8,128]{2,1,0:T(8,128)S(1)}, f32[7,8,128]{2,1,0:T(8,128)S(1)}, u32[]{:S(2)}, u32[]{:S(2)}) collective-permute-start(f32[7,8,128]{2,1,0:T(8,128)S(1)} %get-tuple-element.23.packed), channel_id=1, source_target_pairs={{0,5},{1,4},{2,7},{3,6},{4,1},{5,0},{6,3},{7,2},{8,13},{9,12},{10,... | collective-permute-start | bytes 86024 | tf_op jit(solution)/shard_map/ppermute | solution.py:520
  12.2 2.0 %collective-permute-done.4.got = f32[7,8,128]{2,1,0:T(8,128)S(1)} collective-permute-done((f32[7,8,128]{2,1,0:T(8,128)S(1)}, f32[7,8,128]{2,1,0:T(8,128)S(1)}, u32[]{:S(2)}, u32[]{:S(2)}) %collective-permute-start.4) | collective-permute-done | bytes 28704 | tf_op jit(solution)/shard_map/ppermute | solution.py:520
  14.2 2.3 %collective-permute-start.5 = (f32[6,8,128]{2,1,0:T(8,128)S(1)}, f32[6,8,128]{2,1,0:T(8,128)S(1)}, u32[]{:S(2)}, u32[]{:S(2)}) collective-permute-start(f32[6,8,128]{2,1,0:T(8,128)S(1)} %get-tuple-element.27.message), channel_id=1, source_target_pairs={{0,6},{1,7},{2,4},{3,5},{4,2},{5,3},{6,0},{7,1},{8,14},{9,15},{10,... | collective-permute-start | bytes 73736 | tf_op jit(solution)/shard_map/ppermute | solution.py:520
  16.5 0.6 %shard_map.55.near_a = f32[2,8,128]{2,1,0:T(8,128)S(1)} custom-call(f32[7,8,128]{2,1,0:T(8,128)S(1)} %get-tuple-element.18.own), custom_call_target="tpu_custom_call" | custom-call | flops 4000000 | bytes 65536 | tf_op jit(solution)/shard_map/pallas_call | solution.py:33
  17.2 1.4 %shard_map.56.near_b = f32[2,8,128]{2,1,0:T(8,128)S(1)} custom-call(f32[7,8,128]{2,1,0:T(8,128)S(1)} %get-tuple-element.18.own), custom_call_target="tpu_custom_call" | custom-call | flops 9000000 | bytes 65536 | tf_op jit(solution)/shard_map/pallas_call | solution.py:33
  18.6 1.4 %shard_map.57.near_c = f32[2,8,128]{2,1,0:T(8,128)S(1)} custom-call(f32[7,8,128]{2,1,0:T(8,128)S(1)} %get-tuple-element.18.own, f32[7,8,128]{2,1,0:T(8,128)S(1)} %collective-permute-done.partner), custom_call_target="tpu_custom_call" | custom-call | flops 9000000 | bytes 65536 | tf_op jit(solution)/shard_map/pallas_call | solution.py:33
  20.0 0.8 %shard_map.58.near_d = f32[2,8,128]{2,1,0:T(8,128)S(1)} custom-call(f32[7,8,128]{2,1,0:T(8,128)S(1)} %get-tuple-element.18.own, f32[3,8,128]{2,1,0:T(8,128)S(1)} %get-tuple-element.28.ring), custom_call_target="tpu_custom_call" | custom-call | flops 5000000 | bytes 65536 | tf_op jit(solution)/shard_map/pallas_call | solution.py:33
  20.8 0.7 %shard_map.54 = (f32[2,8,128]{2,1,0:T(8,128)S(1)}, f32[2,32,128]{2,1,0:T(8,128)S(1)}, f32[4,128,128]{2,1,0:T(8,128)S(1)}, bf16[128,1024]{1,0:T(8,128)(2,1)S(1)}) custom-call(f32[7,8,128]{2,1,0:T(8,128)S(1)} %get-tuple-element.18.own, f32[3,4,128]{2,1,0:T(4,128)S(1)} %get-tuple-element.24.close, f32[64,1024]{1,0:T(8,128)S(1)} %get-tuple-element.25.y_wave), custom_call_target="tpu_custom_call" | custom-call | flops 3000000 | bytes 65536 | tf_op jit(solution)/shard_map/pallas_call | solution.py:33
  21.5 0.0 collective-permute-done.5.got.last
  21.5 1.1 %shard_map.59 = (f32[2,2,4,128]{3,2,1,0:T(4,128)}, f32[2,2,4,128]{3,2,1,0:T(4,128)}) custom-call(f32[4,8,128]{2,1,0:T(8,128)S(1)} %get-tuple-element.17.kept, f32[7,8,128]{2,1,0:T(8,128)S(1)} %get-tuple-element.18.own, f32[64,1024]{1,0:T(8,128)S(1)} %get-tuple-element.19.x_table, bf16[128,1024]{1,0:T(8,128)(2,1)S(1)} %get-tuple-element.26.y_table, ...), custom_call_target="tpu_custom_call" | custom-call | flops 4000000 | bytes 65536 | tf_op jit(solution)/shard_map/pallas_call | solution.py:33
  (6 shorter events, 0.1 us)
Async XLA Ops:
  0.6 0.7 %copy-start = (f32[2,2,4,128]{3,2,1,0:T(4,128)S(1)}, f32[2,2,4,128]{3,2,1,0:T(4,128)}, u32[]{:S(2)}) copy-start(f32[2,2,4,128]{3,2,1,0:T(4,128)} %offsets.1) | copy-start | bytes 24580
  0.6 0.7 %copy-start.1 = (f32[2,4,128]{2,1,0:T(4,128)S(1)}, f32[2,4,128]{2,1,0:T(4,128)}, u32[]{:S(2)}) copy-start(f32[2,4,128]{2,1,0:T(4,128)} %circ.1) | copy-start | bytes 12292
  0.7 0.7 %copy-start.2 = (s32[2,4]{1,0:T(2,128)S(1)}, s32[2,4]{1,0:T(2,128)}, u32[]{:S(2)}) copy-start(s32[2,4]{1,0:T(2,128)} %counts.1) | copy-start | bytes 100
  1.8 1.4 %collective-permute-start = (f32[7,8,128]{2,1,0:T(8,128)S(1)}, f32[7,8,128]{2,1,0:T(8,128)S(1)}, u32[]{:S(2)}, u32[]{:S(2)}) collective-permute-start(f32[7,8,128]{2,1,0:T(8,128)S(1)} %get-tuple-element.18.own), channel_id=1, source_target_pairs={{0,4},{1,5},{2,6},{3,7},{4,0},{5,1},{6,2},{7,3},{8,12},{9,13},{10,... | collective-permute-start | bytes 86024 | tf_op jit(solution)/shard_map/ppermute | solution.py:520
  3.2 7.6 %collective-permute-start.1 = (f32[6,8,128]{2,1,0:T(8,128)S(1)}, f32[6,8,128]{2,1,0:T(8,128)S(1)}, u32[]{:S(2)}, u32[]{:S(2)}) collective-permute-start(f32[6,8,128]{2,1,0:T(8,128)S(1)} %get-tuple-element.20.message), channel_id=1, source_target_pairs={{0,12},{1,13},{2,14},{3,15},{4,8},{5,9},{6,10},{7,11},{8,4},{9,5},... | collective-permute-start | bytes 73736 | tf_op jit(solution)/shard_map/ppermute | solution.py:520
  5.9 4.9 %collective-permute-start.2 = (f32[6,8,128]{2,1,0:T(8,128)S(1)}, f32[6,8,128]{2,1,0:T(8,128)S(1)}, u32[]{:S(2)}, u32[]{:S(2)}) collective-permute-start(f32[6,8,128]{2,1,0:T(8,128)S(1)} %get-tuple-element.21), channel_id=1, source_target_pairs={{0,28},{1,29},{2,30},{3,31},{4,24},{5,25},{6,26},{7,27},{8,20},{9,... | collective-permute-start | bytes 73736 | tf_op jit(solution)/shard_map/ppermute | solution.py:520
  7.3 3.5 %collective-permute-start.3 = (f32[4,8,128]{2,1,0:T(8,128)S(1)}, f32[4,8,128]{2,1,0:T(8,128)S(1)}, u32[]{:S(2)}, u32[]{:S(2)}) collective-permute-start(f32[4,8,128]{2,1,0:T(8,128)S(1)} %get-tuple-element.22), channel_id=1, source_target_pairs={{0,20},{1,21},{2,22},{3,23},{4,16},{5,17},{6,18},{7,19},{8,28},{9,... | collective-permute-start | bytes 49160 | tf_op jit(solution)/shard_map/ppermute | solution.py:520
  10.9 3.4 %collective-permute-start.4 = (f32[7,8,128]{2,1,0:T(8,128)S(1)}, f32[7,8,128]{2,1,0:T(8,128)S(1)}, u32[]{:S(2)}, u32[]{:S(2)}) collective-permute-start(f32[7,8,128]{2,1,0:T(8,128)S(1)} %get-tuple-element.23.packed), channel_id=1, source_target_pairs={{0,5},{1,4},{2,7},{3,6},{4,1},{5,0},{6,3},{7,2},{8,13},{9,12},{10,... | collective-permute-start | bytes 86024 | tf_op jit(solution)/shard_map/ppermute | solution.py:520
  14.2 7.2 %collective-permute-start.5 = (f32[6,8,128]{2,1,0:T(8,128)S(1)}, f32[6,8,128]{2,1,0:T(8,128)S(1)}, u32[]{:S(2)}, u32[]{:S(2)}) collective-permute-start(f32[6,8,128]{2,1,0:T(8,128)S(1)} %get-tuple-element.27.message), channel_id=1, source_target_pairs={{0,6},{1,7},{2,4},{3,5},{4,2},{5,3},{6,0},{7,1},{8,14},{9,15},{10,... | collective-permute-start | bytes 73736 | tf_op jit(solution)/shard_map/ppermute | solution.py:520
where the time goes:
time: 22.8 us; the launch traced here: 22.6 us
  starting transfers between devices  8.39 us (37%)
  Pallas kernels  6.42 us (28%)
  waiting for transfers between devices  6.3 us (28%)
  between operations  0.72 us (3%)
  local copies, waits for them, and re-layouts  0.68 us (3%)
    ppermute x6, starting transfers between devices, swap(): return lax.ppermute(message, ('tx', 'ty'), pairs)  8.39 us
    pallas_call x10, Pallas kernels, call(): pl.pallas_call(body, out_shape=outs, in_specs=[VMEM] * len(args), out_spe...  6.42 us
    ppermute x6, waiting for transfers between devices, swap(): return lax.ppermute(message, ('tx', 'ty'), pairs)  6.3 us
    unnamed x6, local copies, waits for them, and re-layouts  0.61 us
  transfers between devices with their start and end apart: 6, of which 3 were waited for; matrix products, arithmetic and copies ran while one was open for 0% of the time, Pallas kernels for 22%

commit v1 on v0

--- a/solution.py
+++ b/solution.py
@@ -70,7 +70,7 @@
 
 
 def moments_kernel(
-    rows, cols, cell_count, corner, offsets, counts, circ, own, kept, x_table, y_table,
+    rows, cols, cell_count, corner_x, corner_y, offsets, counts, circ, own, kept, x_table, y_table,
     powers, amounts,
 ):
     cells = rows * cols
@@ -92,8 +92,8 @@
             kept[3, pl.ds(r * cols + c, 1), :] = jnp.where(slot < count, 1.0, 0.0)
         kept[2, cells_of, :] = jnp.where(kept[3, cells_of, :] > 0.5, circ[r], 0.0)
     off_x, off_y, strength = kept[0], kept[1], kept[2]
-    x_turn = ((corner[pl.ds(0, 1), :] + col_in.astype(jnp.float32)) + off_x) / cell_count
-    y_turn = ((corner[pl.ds(1, 1), :] + row_in.astype(jnp.float32)) + off_y) / cell_count
+    x_turn = ((corner_x[...] + col_in).astype(jnp.float32) + off_x) / cell_count
+    y_turn = ((corner_y[...] + row_in).astype(jnp.float32) + off_y) / cell_count
     own[4] = unit * (col_in.astype(jnp.float32) + off_x)
     own[5] = unit * ((place[2] * rows + row_in).astype(jnp.float32) + off_y)
     own[6] = strength * (unit * cell_count / two_pi)
@@ -493,8 +493,8 @@
     turned = [pltpu.VMEM((slots, 128), f32)]
     near_shape = [((2, cells, slots), f32)]
 
-    first_cell = jnp.stack([ty * cols, tx * rows, tx]).astype(jnp.int32)
-    corner = jnp.broadcast_to(first_cell[:, None], (3, slots)).astype(f32)
+    corner_x = jnp.full((1, slots), ty * cols, jnp.int32)
+    corner_y = jnp.full((1, slots), tx * rows, jnp.int32)
     own, kept, x_table, y_wave = call(
         functools.partial(moments_kernel, rows, cols, cell_count),
         [
@@ -508,7 +508,7 @@
             pltpu.VMEM((cells, slots), f32),
         ],
         4_000_000,
-        corner, offsets, counts, circ,
+        corner_x, corner_y, offsets, counts, circ,
     )
 
     def swap(message, chip_bit, column_bit, flip=True):

time: 22.8 us -> 22.7 us (level)
  no operation moved by 1% of the time
where the time goes in v1:
time: 22.7 us; the launch traced here: 22.5 us
  starting transfers between devices  8.38 us (37%)
  Pallas kernels  6.43 us (28%)
  waiting for transfers between devices  6.31 us (28%)
  between operations  0.74 us (3%)
  local copies, waits for them, and re-layouts  0.67 us (3%)
    ppermute x6, starting transfers between devices, swap(): return lax.ppermute(message, ('tx', 'ty'), pairs)  8.38 us
    pallas_call x10, Pallas kernels, call(): pl.pallas_call(body, out_shape=outs, in_specs=[VMEM] * len(args), out_spe...  6.43 us
    ppermute x6, waiting for transfers between devices, swap(): return lax.ppermute(message, ('tx', 'ty'), pairs)  6.31 us
    unnamed x6, local copies, waits for them, and re-layouts  0.66 us
  transfers between devices with their start and end apart: 6, of which 3 were waited for; matrix products, arithmetic and copies ran while one was open for 0% of the time, Pallas kernels for 22%

profile of v1, /device:TPU:0, one launch (start us, length us, event | category | flops | bytes accessed | tf_op | source)
XLA Modules:
  0.0 22.5 jit_solution(16726951163219237774)
XLA Ops:
  0.6 0.0 copy-start
  0.7 0.0 copy-start.2
  0.7 0.6 %copy-done = f32[2,2,4,128]{3,2,1,0:T(4,128)S(1)} copy-done((f32[2,2,4,128]{3,2,1,0:T(4,128)S(1)}, f32[2,2,4,128]{3,2,1,0:T(4,128)}, u32[]{:S(2)}) %copy-start) | copy-done | bytes 8216
  1.3 0.0 copy-done.1
  1.3 0.0 copy-done.2
  1.3 0.4 %shard_map.50 = (f32[7,8,128]{2,1,0:T(8,128)S(1)}, f32[4,8,128]{2,1,0:T(8,128)S(1)}, f32[64,1024]{1,0:T(8,128)S(1)}, f32[64,1024]{1,0:T(8,128)S(1)}) custom-call(s32[1,128]{1,0:T(1,128)S(1)} %broadcast_in_dim.6.corner_x, s32[1,128]{1,0:T(1,128)S(1)} %broadcast_in_dim.7.corner_y, f32[2,2,4,128]{3,2,1,0:T(4,128)S(1)} %copy-done, s32[2,4]{1,0:T(2,128)S(1)} %copy-done.2, ...), custom_call_target="tpu_custom_call" | custom-call | flops 4000000 | bytes 65536 | tf_op jit(solution)/shard_map/pallas_call | solution.py:33
  1.7 0.6 %collective-permute-start = (f32[7,8,128]{2,1,0:T(8,128)S(1)}, f32[7,8,128]{2,1,0:T(8,128)S(1)}, u32[]{:S(2)}, u32[]{:S(2)}) collective-permute-start(f32[7,8,128]{2,1,0:T(8,128)S(1)} %get-tuple-element.18.own), channel_id=1, source_target_pairs={{0,4},{1,5},{2,6},{3,7},{4,0},{5,1},{6,2},{7,3},{8,12},{9,13},{10,... | collective-permute-start | bytes 86024 | tf_op jit(solution)/shard_map/ppermute | solution.py:520
  2.3 0.9 %collective-permute-done.partner = f32[7,8,128]{2,1,0:T(8,128)S(1)} collective-permute-done((f32[7,8,128]{2,1,0:T(8,128)S(1)}, f32[7,8,128]{2,1,0:T(8,128)S(1)}, u32[]{:S(2)}, u32[]{:S(2)}) %collective-permute-start) | collective-permute-done | bytes 28704 | tf_op jit(solution)/shard_map/ppermute | solution.py:520
  3.2 2.7 %collective-permute-start.1 = (f32[6,8,128]{2,1,0:T(8,128)S(1)}, f32[6,8,128]{2,1,0:T(8,128)S(1)}, u32[]{:S(2)}, u32[]{:S(2)}) collective-permute-start(f32[6,8,128]{2,1,0:T(8,128)S(1)} %get-tuple-element.20.message), channel_id=1, source_target_pairs={{0,12},{1,13},{2,14},{3,15},{4,8},{5,9},{6,10},{7,11},{8,4},{9,5},... | collective-permute-start | bytes 73736 | tf_op jit(solution)/shard_map/ppermute | solution.py:520
  5.8 1.4 %collective-permute-start.2 = (f32[6,8,128]{2,1,0:T(8,128)S(1)}, f32[6,8,128]{2,1,0:T(8,128)S(1)}, u32[]{:S(2)}, u32[]{:S(2)}) collective-permute-start(f32[6,8,128]{2,1,0:T(8,128)S(1)} %get-tuple-element.21), channel_id=1, source_target_pairs={{0,28},{1,29},{2,30},{3,31},{4,24},{5,25},{6,26},{7,27},{8,20},{9,... | collective-permute-start | bytes 73736 | tf_op jit(solution)/shard_map/ppermute | solution.py:520
  7.3 0.0 collective-permute-start.3
  7.3 3.4 %collective-permute-done.3.others_1_ = f32[4,8,128]{2,1,0:T(8,128)S(1)} collective-permute-done((f32[4,8,128]{2,1,0:T(8,128)S(1)}, f32[4,8,128]{2,1,0:T(8,128)S(1)}, u32[]{:S(2)}, u32[]{:S(2)}) %collective-permute-start.3) | collective-permute-done | bytes 16416 | tf_op jit(solution)/shard_map/ppermute | solution.py:520
  10.7 0.0 collective-permute-done.1.near_item.others_0_
  10.8 0.0 collective-permute-done.2.far_item.others_2_
  10.8 1.4 %collective-permute-start.4 = (f32[7,8,128]{2,1,0:T(8,128)S(1)}, f32[7,8,128]{2,1,0:T(8,128)S(1)}, u32[]{:S(2)}, u32[]{:S(2)}) collective-permute-start(f32[7,8,128]{2,1,0:T(8,128)S(1)} %get-tuple-element.23.packed), channel_id=1, source_target_pairs={{0,5},{1,4},{2,7},{3,6},{4,1},{5,0},{6,3},{7,2},{8,13},{9,12},{10,... | collective-permute-start | bytes 86024 | tf_op jit(solution)/shard_map/ppermute | solution.py:520
  12.2 2.0 %collective-permute-done.4.got = f32[7,8,128]{2,1,0:T(8,128)S(1)} collective-permute-done((f32[7,8,128]{2,1,0:T(8,128)S(1)}, f32[7,8,128]{2,1,0:T(8,128)S(1)}, u32[]{:S(2)}, u32[]{:S(2)}) %collective-permute-start.4) | collective-permute-done | bytes 28704 | tf_op jit(solution)/shard_map/ppermute | solution.py:520
  14.2 2.3 %collective-permute-start.5 = (f32[6,8,128]{2,1,0:T(8,128)S(1)}, f32[6,8,128]{2,1,0:T(8,128)S(1)}, u32[]{:S(2)}, u32[]{:S(2)}) collective-permute-start(f32[6,8,128]{2,1,0:T(8,128)S(1)} %get-tuple-element.27.message), channel_id=1, source_target_pairs={{0,6},{1,7},{2,4},{3,5},{4,2},{5,3},{6,0},{7,1},{8,14},{9,15},{10,... | collective-permute-start | bytes 73736 | tf_op jit(solution)/shard_map/ppermute | solution.py:520
  16.5 0.6 %shard_map.55.near_a = f32[2,8,128]{2,1,0:T(8,128)S(1)} custom-call(f32[7,8,128]{2,1,0:T(8,128)S(1)} %get-tuple-element.18.own), custom_call_target="tpu_custom_call" | custom-call | flops 4000000 | bytes 65536 | tf_op jit(solution)/shard_map/pallas_call | solution.py:33
  17.1 1.4 %shard_map.56.near_b = f32[2,8,128]{2,1,0:T(8,128)S(1)} custom-call(f32[7,8,128]{2,1,0:T(8,128)S(1)} %get-tuple-element.18.own), custom_call_target="tpu_custom_call" | custom-call | flops 9000000 | bytes 65536 | tf_op jit(solution)/shard_map/pallas_call | solution.py:33
  18.6 1.4 %shard_map.57.near_c = f32[2,8,128]{2,1,0:T(8,128)S(1)} custom-call(f32[7,8,128]{2,1,0:T(8,128)S(1)} %get-tuple-element.18.own, f32[7,8,128]{2,1,0:T(8,128)S(1)} %collective-permute-done.partner), custom_call_target="tpu_custom_call" | custom-call | flops 9000000 | bytes 65536 | tf_op jit(solution)/shard_map/pallas_call | solution.py:33
  20.0 0.8 %shard_map.58.near_d = f32[2,8,128]{2,1,0:T(8,128)S(1)} custom-call(f32[7,8,128]{2,1,0:T(8,128)S(1)} %get-tuple-element.18.own, f32[3,8,128]{2,1,0:T(8,128)S(1)} %get-tuple-element.28.ring), custom_call_target="tpu_custom_call" | custom-call | flops 5000000 | bytes 65536 | tf_op jit(solution)/shard_map/pallas_call | solution.py:33
  20.7 0.7 %shard_map.54 = (f32[2,8,128]{2,1,0:T(8,128)S(1)}, f32[2,32,128]{2,1,0:T(8,128)S(1)}, f32[4,128,128]{2,1,0:T(8,128)S(1)}, bf16[128,1024]{1,0:T(8,128)(2,1)S(1)}) custom-call(f32[7,8,128]{2,1,0:T(8,128)S(1)} %get-tuple-element.18.own, f32[3,4,128]{2,1,0:T(4,128)S(1)} %get-tuple-element.24.close, f32[64,1024]{1,0:T(8,128)S(1)} %get-tuple-element.25.y_wave), custom_call_target="tpu_custom_call" | custom-call | flops 3000000 | bytes 65536 | tf_op jit(solution)/shard_map/pallas_call | solution.py:33
  21.4 0.0 collective-permute-done.5.got.last
  21.4 1.1 %shard_map.59 = (f32[2,2,4,128]{3,2,1,0:T(4,128)}, f32[2,2,4,128]{3,2,1,0:T(4,128)}) custom-call(f32[4,8,128]{2,1,0:T(8,128)S(1)} %get-tuple-element.17.kept, f32[7,8,128]{2,1,0:T(8,128)S(1)} %get-tuple-element.18.own, f32[64,1024]{1,0:T(8,128)S(1)} %get-tuple-element.19.x_table, bf16[128,1024]{1,0:T(8,128)(2,1)S(1)} %get-tuple-element.26.y_table, ...), custom_call_target="tpu_custom_call" | custom-call | flops 4000000 | bytes 65536 | tf_op jit(solution)/shard_map/pallas_call | solution.py:33
  (6 shorter events, 0.1 us)
Async XLA Ops:
  0.6 0.7 %copy-start = (f32[2,2,4,128]{3,2,1,0:T(4,128)S(1)}, f32[2,2,4,128]{3,2,1,0:T(4,128)}, u32[]{:S(2)}) copy-start(f32[2,2,4,128]{3,2,1,0:T(4,128)} %offsets.1) | copy-start | bytes 24580
  0.6 0.7 %copy-start.1 = (f32[2,4,128]{2,1,0:T(4,128)S(1)}, f32[2,4,128]{2,1,0:T(4,128)}, u32[]{:S(2)}) copy-start(f32[2,4,128]{2,1,0:T(4,128)} %circ.1) | copy-start | bytes 12292
  0.7 0.7 %copy-start.2 = (s32[2,4]{1,0:T(2,128)S(1)}, s32[2,4]{1,0:T(2,128)}, u32[]{:S(2)}) copy-start(s32[2,4]{1,0:T(2,128)} %counts.1) | copy-start | bytes 100
  1.7 1.4 %collective-permute-start = (f32[7,8,128]{2,1,0:T(8,128)S(1)}, f32[7,8,128]{2,1,0:T(8,128)S(1)}, u32[]{:S(2)}, u32[]{:S(2)}) collective-permute-start(f32[7,8,128]{2,1,0:T(8,128)S(1)} %get-tuple-element.18.own), channel_id=1, source_target_pairs={{0,4},{1,5},{2,6},{3,7},{4,0},{5,1},{6,2},{7,3},{8,12},{9,13},{10,... | collective-permute-start | bytes 86024 | tf_op jit(solution)/shard_map/ppermute | solution.py:520
  3.2 7.6 %collective-permute-start.1 = (f32[6,8,128]{2,1,0:T(8,128)S(1)}, f32[6,8,128]{2,1,0:T(8,128)S(1)}, u32[]{:S(2)}, u32[]{:S(2)}) collective-permute-start(f32[6,8,128]{2,1,0:T(8,128)S(1)} %get-tuple-element.20.message), channel_id=1, source_target_pairs={{0,12},{1,13},{2,14},{3,15},{4,8},{5,9},{6,10},{7,11},{8,4},{9,5},... | collective-permute-start | bytes 73736 | tf_op jit(solution)/shard_map/ppermute | solution.py:520
  5.8 4.9 %collective-permute-start.2 = (f32[6,8,128]{2,1,0:T(8,128)S(1)}, f32[6,8,128]{2,1,0:T(8,128)S(1)}, u32[]{:S(2)}, u32[]{:S(2)}) collective-permute-start(f32[6,8,128]{2,1,0:T(8,128)S(1)} %get-tuple-element.21), channel_id=1, source_target_pairs={{0,28},{1,29},{2,30},{3,31},{4,24},{5,25},{6,26},{7,27},{8,20},{9,... | collective-permute-start | bytes 73736 | tf_op jit(solution)/shard_map/ppermute | solution.py:520
  7.3 3.5 %collective-permute-start.3 = (f32[4,8,128]{2,1,0:T(8,128)S(1)}, f32[4,8,128]{2,1,0:T(8,128)S(1)}, u32[]{:S(2)}, u32[]{:S(2)}) collective-permute-start(f32[4,8,128]{2,1,0:T(8,128)S(1)} %get-tuple-element.22), channel_id=1, source_target_pairs={{0,20},{1,21},{2,22},{3,23},{4,16},{5,17},{6,18},{7,19},{8,28},{9,... | collective-permute-start | bytes 49160 | tf_op jit(solution)/shard_map/ppermute | solution.py:520
  10.8 3.4 %collective-permute-start.4 = (f32[7,8,128]{2,1,0:T(8,128)S(1)}, f32[7,8,128]{2,1,0:T(8,128)S(1)}, u32[]{:S(2)}, u32[]{:S(2)}) collective-permute-start(f32[7,8,128]{2,1,0:T(8,128)S(1)} %get-tuple-element.23.packed), channel_id=1, source_target_pairs={{0,5},{1,4},{2,7},{3,6},{4,1},{5,0},{6,3},{7,2},{8,13},{9,12},{10,... | collective-permute-start | bytes 86024 | tf_op jit(solution)/shard_map/ppermute | solution.py:520
  14.2 7.2 %collective-permute-start.5 = (f32[6,8,128]{2,1,0:T(8,128)S(1)}, f32[6,8,128]{2,1,0:T(8,128)S(1)}, u32[]{:S(2)}, u32[]{:S(2)}) collective-permute-start(f32[6,8,128]{2,1,0:T(8,128)S(1)} %get-tuple-element.27.message), channel_id=1, source_target_pairs={{0,6},{1,7},{2,4},{3,5},{4,2},{5,3},{6,0},{7,1},{8,14},{9,15},{10,... | collective-permute-start | bytes 73736 | tf_op jit(solution)/shard_map/ppermute | solution.py:520
